TPU v7x, 128 devices: a whole 4x4x4 slice. The times are simulated.
128 devices in a mesh: row: 8 (over y_hi, x), col: 16 (over z, y_lo, core).
Axes of the slice: x: 4, y: 4 (y_hi: 2, y_lo: 2; y = y_hi * 2 + y_lo), z: 4, core: 2. Of those that a mesh axis runs over, the one named last changes fastest.
Arguments:
- features: bfloat16 [64, 1024, 1024], P(None, 'col', 'row'), may hold values from -120 to 120
- conv_first: bfloat16 [9, 64, 64], replicated, may hold values from -0.25 to 0.25
- conv_second: bfloat16 [9, 64, 64], replicated, may hold values from -0.25 to 0.25
- head_weight: bfloat16 [37, 64], replicated, may hold values from -0.75 to 0.75
- head_bias: float32 [37], replicated, may hold values from -4 to 4
- cotangent: bfloat16 [37, 1024, 1024], P(None, 'col', 'row'), may hold values from -6 to 6
Outputs:
- logits: bfloat16 [37, 1024, 1024], P(None, 'col', 'row')
- input_grad: bfloat16 [64, 1024, 1024], P(None, 'col', 'row')
- grad_first: float32 [9, 64, 64], replicated
- grad_second: float32 [9, 64, 64], replicated
- grad_head: float32 [37, 64], replicated
- grad_bias: float32 [37], replicated
All inputs are finite; a program needn't handle non-finite values.
Results may differ from a plain program's by a relative error of at most 0.007.
Values may be sent and summed in bfloat16 or wider, within the bound.
No kernel may reach another device: no remote copies, remote signals or barrier semaphores. Data moves between devices by JAX's collectives and lax.ppermute only.
A program may use at most 128 MiB of HBM per device.

v0:
```python
import jax
import jax.numpy as jnp
from jax import lax
from jax.sharding import PartitionSpec as P

DILATION_STEP = 16
epsilon = 1e-05


def with_halo(block, sides, width):
    for axis, dim in sides:
        count = lax.axis_size(axis)
        forward = [(i, i + 1) for i in range(count - 1)]
        backward = [(target, source) for source, target in forward]
        low = lax.ppermute(
            lax.slice_in_dim(block, block.shape[dim] - width, None, axis=dim), axis, forward
        )
        high = lax.ppermute(lax.slice_in_dim(block, 0, width, axis=dim), axis, backward)
        block = jnp.concatenate([low, block, high], axis=dim)
    return block


def as_sent(shard):

    def short(part):
        return part.astype(jnp.bfloat16) if part.dtype == jnp.float32 else part

    return jax.tree.map(short, shard)


def elu_apply(value_entries):
    return jnp.where(
        value_entries > 0, value_entries, jnp.exp(jnp.minimum(value_entries, 0.0)) - 1.0
    )


def elu_slope(value_entries):
    return jnp.where(value_entries > 0, 1.0, jnp.exp(jnp.minimum(value_entries, 0.0)))


def widen(value_entries):
    return with_halo(value_entries, (("row", 2), ("col", 1)), DILATION_STEP)


def widen_grad(value_entries):
    return with_halo(value_entries, (("row", 2), ("col", 1)), DILATION_STEP)


def tap_window(padded, kernel_row, kernel_column, adjoint, col_count, row_count):
    shift_direction = -1 if adjoint else 1
    column_shift = DILATION_STEP + shift_direction * DILATION_STEP * (kernel_column - 1)
    row_shift = DILATION_STEP + shift_direction * DILATION_STEP * (kernel_row - 1)
    window = padded[:, column_shift : column_shift + col_count, row_shift : row_shift + row_count]
    return window.reshape(padded.shape[0], col_count * row_count)


def convolve(padded, weights, col_count, row_count, adjoint):
    running = jnp.zeros((weights.shape[1], col_count * row_count), jnp.float32)
    for kernel_row in range(3):
        for kernel_column in range(3):
            window = tap_window(padded, kernel_row, kernel_column, adjoint, col_count, row_count)
            matrix = weights[3 * kernel_row + kernel_column]
            if adjoint:
                matrix = matrix.T
            running = running + jnp.dot(matrix, window, preferred_element_type=jnp.float32)
    return running.reshape(-1, col_count, row_count)


def weight_terms(gradient, padded, col_count, row_count):
    flattened = gradient.reshape(gradient.shape[0], -1)
    collected = []
    for kernel_row in range(3):
        for kernel_column in range(3):
            window = tap_window(padded, kernel_row, kernel_column, False, col_count, row_count)
            collected.append(
                lax.dot_general(
                    flattened, window, (((1,), (1,)), ((), ())), preferred_element_type=jnp.float32
                )
            )
    return jnp.stack(collected, 0)


def normalize(activation, cell_count):
    totals = lax.psum(jnp.sum(activation, axis=(1, 2)), ("row", "col"))
    average = totals / cell_count
    centered = activation - average[:, None, None]
    spread = lax.psum(jnp.sum(centered * centered, axis=(1, 2)), ("row", "col")) / cell_count
    inverse_std = lax.rsqrt(spread + epsilon)
    return (centered * inverse_std[:, None, None], inverse_std)


def norm_back(gradient, normed, inverse_std, cell_count):
    first_sum, second_sum = lax.psum(
        (jnp.sum(gradient, axis=(1, 2)), jnp.sum(gradient * normed, axis=(1, 2))), ("row", "col")
    )
    first_mean = first_sum / cell_count
    second_mean = second_sum / cell_count
    return inverse_std[:, None, None] * (
        gradient - first_mean[:, None, None] - normed * second_mean[:, None, None]
    )


def mirror_prepare(tensor, col_devices):
    planes, col_count, row_count = tensor.shape
    slab_rows = row_count // col_devices
    shaped = tensor.reshape(planes, col_count, col_devices, slab_rows).transpose(2, 1, 0, 3)
    return shaped.reshape(col_devices, col_count, planes * slab_rows)


def mirror_middle(received):
    return received.reshape(received.shape[1], 1, received.shape[2])


def mirror_tail(received, col_devices, row_devices):
    return received.reshape(received.shape[0], col_devices, row_devices, received.shape[2])


def mirror_finish(received, planes, row_devices):
    row_count = received.shape[0]
    slab_rows = received.shape[3] // planes
    shaped = received.reshape(row_count, row_devices, planes, slab_rows).transpose(2, 1, 3, 0)
    return shaped.reshape(planes, row_devices * slab_rows, row_count)


def mirror_half(tensors):
    col_devices = lax.axis_size("col")
    row_devices = lax.axis_size("row")
    planes = tuple((member.shape[0] for member in tensors))
    first = lax.all_to_all(
        as_sent(tuple((mirror_prepare(member, col_devices) for member in tensors))),
        "col",
        split_axis=0,
        concat_axis=1,
        tiled=True,
    )
    second = lax.all_to_all(
        as_sent(tuple((mirror_middle(member) for member in first))),
        ("row", "col"),
        split_axis=0,
        concat_axis=1,
        tiled=True,
    )
    third = lax.all_to_all(
        as_sent(tuple((mirror_tail(member, col_devices, row_devices) for member in second))),
        "col",
        split_axis=1,
        concat_axis=0,
        tiled=True,
    )
    return tuple(
        (
            mirror_finish(member, count_planes, row_devices)
            for member, count_planes in zip(third, planes)
        )
    )


def mirror_full(tensors):
    col_devices = lax.axis_size("col")
    row_devices = lax.axis_size("row")
    planes = tuple((member.shape[0] for member in tensors))
    first = lax.all_to_all(
        tuple((mirror_prepare(member, col_devices) for member in tensors)),
        "col",
        split_axis=0,
        concat_axis=1,
        tiled=True,
    )
    second = lax.all_to_all(
        tuple((mirror_middle(member) for member in first)),
        ("row", "col"),
        split_axis=0,
        concat_axis=1,
        tiled=True,
    )
    third = lax.all_to_all(
        tuple((mirror_tail(member, col_devices, row_devices) for member in second)),
        "col",
        split_axis=1,
        concat_axis=0,
        tiled=True,
    )
    return tuple(
        (
            mirror_finish(member, count_planes, row_devices)
            for member, count_planes in zip(third, planes)
        )
    )


def on_device(features, conv_first, conv_second, head_weight, head_bias, cotangent):
    channels, col_count, row_count = features.shape
    length = col_count * lax.axis_size("col")
    cell_count = float(length * length)
    cot_mirror = mirror_half((cotangent,))[0]
    wide_in = widen(features)
    act_first = convolve(wide_in, conv_first, col_count, row_count, False)
    normed_first, inverse_first = normalize(act_first, cell_count)
    hidden_first = elu_apply(normed_first).astype(jnp.bfloat16)
    wide_hidden = widen(hidden_first)
    act_second = convolve(wide_hidden, conv_second, col_count, row_count, False)
    normed_second, inverse_second = normalize(act_second, cell_count)
    summed = normed_second + features.astype(jnp.float32)
    hidden = elu_apply(summed).astype(jnp.bfloat16)
    flat_hidden = hidden.reshape(channels, -1)
    raw_logits = (
        jnp.dot(head_weight, flat_hidden, preferred_element_type=jnp.float32) + head_bias[:, None]
    ).reshape(-1, col_count, row_count)
    logit_mirror = mirror_full((raw_logits,))[0]
    logits = (0.5 * (raw_logits + logit_mirror)).astype(jnp.bfloat16)
    grad_sym = (0.5 * (cotangent.astype(jnp.float32) + cot_mirror.astype(jnp.float32))).astype(
        jnp.bfloat16
    )
    flat_sym = grad_sym.reshape(grad_sym.shape[0], -1)
    bias_term = jnp.sum(flat_sym, axis=1, dtype=jnp.float32)
    head_term = lax.dot_general(
        flat_sym, flat_hidden, (((1,), (1,)), ((), ())), preferred_element_type=jnp.float32
    )
    grad_hidden = jnp.dot(head_weight.T, flat_sym, preferred_element_type=jnp.float32).reshape(
        channels, col_count, row_count
    )
    grad_summed = grad_hidden * elu_slope(summed)
    grad_act_second = norm_back(grad_summed, normed_second, inverse_second, cell_count).astype(
        jnp.bfloat16
    )
    second_term = weight_terms(grad_act_second, wide_hidden, col_count, row_count)
    grad_hidden_first = convolve(
        widen_grad(grad_act_second), conv_second, col_count, row_count, True
    )
    grad_normed_first = grad_hidden_first * elu_slope(normed_first)
    grad_act_first = norm_back(grad_normed_first, normed_first, inverse_first, cell_count).astype(
        jnp.bfloat16
    )
    first_term = weight_terms(grad_act_first, wide_in, col_count, row_count)
    input_grad = (
        convolve(widen_grad(grad_act_first), conv_first, col_count, row_count, True) + grad_summed
    ).astype(jnp.bfloat16)
    reduced = lax.psum((first_term, second_term, head_term, bias_term), ("row", "col"))
    inverse_len = 1.0 / length
    return (
        logits,
        input_grad,
        reduced[0] * inverse_len,
        reduced[1] * inverse_len,
        reduced[2] * inverse_len,
        reduced[3] * inverse_len,
    )


def solution(mesh):
    placed = (P(None, "col", "row"), P(), P(), P(), P(), P(None, "col", "row"))
    return jax.shard_map(
        on_device,
        mesh=mesh,
        in_specs=placed,
        out_specs=(P(None, "col", "row"), P(None, "col", "row"), P(), P(), P(), P()),
        check_vma=False,
    )
```

profile of v0, /device:TPU:1, one launch (start us, length us, event | category | flops | bytes accessed | tf_op | source)
XLA Modules:
  0.0 945.5 jit_solution(8504347659862040630)
XLA Ops:
  12.6 5.3 collective-permute-start
  21.0 7.8 all-to-all-start.3
  29.6 2.7 copy.225
  32.3 2.7 copy.227
  35.7 3.5 collective-permute-start.2
  45.4 7.2 collective-permute-done.3
  52.6 3.2 maximum_maximum_fusion
  63.5 67.2 %psum.84 = f32[64]{0:T(128)S(1)} all-reduce(f32[64]{0:T(128)S(1)} %get-tuple-element.108), channel_id=1, replica_groups=mesh['row'=8,'col'=16] {'row','col'}, use_global_device_ids=true, to_apply=%region_1.0 | all-reduce | flops 64 | bytes 512 | tf_op jit(solution)/shard_map/psum | solution.py:84
  131.1 63.5 %psum.85 = f32[64]{0:T(128)S(1)} all-reduce(f32[64]{0:T(128)S(1)} %multiply_reduce_fusion.2), channel_id=1, replica_groups=mesh['row'=8,'col'=16] {'row','col'}, use_global_device_ids=true, to_apply=%region_3.0 | all-reduce | flops 64 | bytes 512 | tf_op jit(solution)/shard_map/psum | solution.py:87
  199.3 3.0 collective-permute-start.4
  202.3 2.9 copy.242
  206.5 3.4 copy.243
  209.8 4.3 collective-permute-done.5
  214.1 3.4 copy.244
  217.5 2.8 pad_maximum_fusion.18
  220.2 3.9 collective-permute-start.7
  226.6 3.1 reduce.8
  229.6 3.4 reshape.289
  233.1 11.2 %all-to-all-start.4 = ((bf16[128,2,1184]{2,1,0:T(2,128)(2,1)}), bf16[128,2,1184]{2,1,0:T(2,128)(2,1)}, u32[]{:S(2)}, u32[]{:S(2)}) async-start(bf16[128,2,1184]{2,1,0:T(2,128)(2,1)} %reshape.289), calls=%async_computation.4 | async-start | bytes 1310720 | tf_op jit(solution)/shard_map/all_to_all | solution.py:136
  244.3 2.9 fusion.146
  247.3 4.2 pad_maximum_fusion.1
  260.6 67.2 %psum.86 = f32[64]{0:T(128)S(1)} all-reduce(f32[64]{0:T(128)S(1)} %get-tuple-element.110), channel_id=1, replica_groups=mesh['row'=8,'col'=16] {'row','col'}, use_global_device_ids=true, to_apply=%region_5.6 | all-reduce | flops 64 | bytes 512 | tf_op jit(solution)/shard_map/psum | solution.py:84
  327.7 6.2 reshape.290
  336.5 4.3 all-to-all-start.5
  342.8 65.3 %psum.87 = f32[64]{0:T(128)S(1)} all-reduce(f32[64]{0:T(128)S(1)} %fusion.19), channel_id=1, replica_groups=mesh['row'=8,'col'=16] {'row','col'}, use_global_device_ids=true, to_apply=%region_7.8 | all-reduce | flops 64 | bytes 512 | tf_op jit(solution)/shard_map/psum | solution.py:87
  409.4 12.2 %reshape.288 = f32[128,8,37,8]{3,2,1,0:T(8,128)} reshape(f32[16,8,1,8,296]{4,3,1,0,2:T(8,128)} %convert_bitcast_fusion) | data formatting | bytes 2424832 | tf_op jit(solution)/shard_map/convert_element_type | solution.py:211
  421.5 11.1 %copy.273 = f32[37,8,8,128]{3,2,1,0:T(8,128)S(1)} copy(f32[37,8,8,128]{2,0,1,3:T(8,128)} %bitcast.528) | data formatting | bytes 2424832 | tf_op jit(solution)/shard_map/convert_element_type | solution.py:211
  436.2 3.2 fusion.228
  439.4 62.9 %all-reduce.1 = (f32[64]{0:T(128)S(1)}, f32[64]{0:T(128)S(1)}) all-reduce(f32[64]{0:T(128)S(1)} %get-tuple-element.39, f32[64]{0:T(128)S(1)} %get-tuple-element.38), channel_id=1, replica_groups=mesh['row'=8,'col'=16] {'row','col'}, use_global_device_ids=true, to_apply=%region_11.12 | all-reduce | flops 128 | bytes 1024 | tf_op jit(solution)/shard_map/psum | solution.py:93
  502.3 2.9 multiply_convert_fusion.1
  517.0 2.9 copy.275
  519.9 2.9 copy.276
  524.1 4.7 collective-permute-start.8
  530.4 3.2 fusion.25
  534.9 3.7 copy.258
  538.7 5.1 copy.259
  543.8 3.1 copy.260
  546.9 5.3 all-to-all-start
  552.5 3.4 copy.277
  555.9 3.4 copy.278
  561.2 3.5 collective-permute-start.11
  568.5 8.1 collective-permute-done.11
  576.5 7.2 collective-permute-done.10
  583.7 3.2 maximum_maximum_fusion.2
  592.5 2.5 fusion.227
  595.0 67.2 %all-reduce = (f32[64]{0:T(128)S(1)}, f32[64]{0:T(128)S(1)}, f32[37,64]{1,0:T(8,128)S(1)}, f32[37]{0:T(128)S(1)}) all-reduce(f32[64]{0:T(128)S(1)} %get-tuple-element.37, f32[64]{0:T(128)S(1)} %get-tuple-element.36, f32[37,64]{1,0:T(8,128)S(1)} %convolution_bitcast_fusion.23, ...), channel_id=1, replica_groups=mesh['row'=8,'col'=16] {'row','col'}, use_global_device_ids=true, to_apply=%region_15.16 | all-reduce | flops 2533 | bytes 20264 | tf_op jit(solution)/shard_map/psum | solution.py:93
  662.2 2.7 fusion.10
  673.6 3.0 copy.291
  676.6 2.9 copy.292
  680.8 5.1 collective-permute-start.12
  686.4 3.2 collective-permute-done.12
  689.6 3.4 copy.293
  692.9 3.4 copy.294
  696.3 2.9 pad_maximum_fusion.12
  699.2 4.6 collective-permute-start.15
  708.2 125.5 %all-reduce.5.cloned.1.call-done = (f32[9,64,64]{2,1,0:T(8,128)}, f32[9,64,64]{2,1,0:T(8,128)}) async-done(((f32[9,64,64]{2,1,0:T(8,128)}, f32[9,64,64]{2,1,0:T(8,128)}), (f32[9,64,64]{2,1,0:T(8,128)}, f32[9,64,64]{2,1,0:T(8,128)})) %all-reduce.5.cloned.1.call-update) | async-done | bytes 294928 | tf_op jit(solution)/shard_map/psum | solution.py:238
  837.1 4.8 maximum_maximum_fusion.3
  848.5 4.2 copy.261
  852.7 7.4 all-to-all-start.1
  866.1 17.9 %all-to-all-done.1 = f32[1024,1,296]{2,1,0:T(1,128)} async-done(((f32[1024,1,296]{2,1,0:T(1,128)}), f32[1024,1,296]{2,1,0:T(1,128)}, u32[]{:S(2)}, u32[]{:S(2)}) %all-to-all-start.1) | async-done | bytes 1212448 | tf_op jit(solution)/shard_map/all_to_all | solution.py:169
  887.0 5.5 all-to-all-start.2
  898.6 15.5 %all-to-all-done.2 = f32[8,16,8,296]{3,2,0,1:T(8,128)} async-done(((f32[8,16,8,296]{3,2,0,1:T(8,128)}), f32[8,16,8,296]{3,2,0,1:T(8,128)}, u32[]{:S(2)}, u32[]{:S(2)}) %all-to-all-start.2) | async-done | bytes 1212448 | tf_op jit(solution)/shard_map/all_to_all | solution.py:176
  914.1 12.2 %reshape.287 = f32[128,8,37,8]{3,2,1,0:T(8,128)} reshape(f32[16,8,1,8,296]{4,3,1,0,2:T(8,128)} %bitcast.32) | data formatting | bytes 2424832 | tf_op jit(solution)/shard_map/reshape | solution.py:121
  926.2 11.2 %copy.265 = f32[37,8,8,128]{3,2,1,0:T(8,128)S(1)} copy(f32[37,8,8,128]{2,0,1,3:T(8,128)} %bitcast.529) | data formatting | bytes 2424832 | tf_op jit(solution)/shard_map/transpose | solution.py:121
  (229 shorter events, 118.7 us)
Async XLA Ops:
  7.2 427.7 %copy-start = (bf16[37,64]{1,0:T(8,128)(2,1)S(1)}, bf16[37,64]{1,0:T(8,128)(2,1)}, u32[]{:S(2)}) copy-start(bf16[37,64]{1,0:T(8,128)(2,1)} %param.9) | copy-start | bytes 14212
  9.2 8.7 copy-start.43
  10.3 22.0 %collective-permute-start.1 = (bf16[64,64,16]{1,2,0:T(8,128)(2,1)}, bf16[64,64,16]{1,2,0:T(8,128)(2,1)}, u32[]{:S(2)}, u32[]{:S(2)}) collective-permute-start(bf16[64,64,16]{1,2,0:T(8,128)(2,1)} %copy.320), channel_id=1, source_target_pairs={{16,0},{32,16},{48,32},{64,48},{80,64},{96,80},{112,96},{17,1},{33... | collective-permute-start | bytes 393224 | tf_op jit(solution)/shard_map/ppermute | solution.py:18
  12.6 16.9 %collective-permute-start = (bf16[64,64,16]{1,2,0:T(8,128)(2,1)}, bf16[64,64,16]{1,2,0:T(8,128)(2,1)}, u32[]{:S(2)}, u32[]{:S(2)}) collective-permute-start(bf16[64,64,16]{1,2,0:T(8,128)(2,1)} %copy.319), channel_id=1, source_target_pairs={{0,16},{16,32},{32,48},{48,64},{64,80},{80,96},{96,112},{1,17},{17... | collective-permute-start | bytes 393224 | tf_op jit(solution)/shard_map/ppermute | solution.py:15
  19.6 9.2 copy-start.15
  21.0 205.0 %all-to-all-start.3 = ((bf16[16,64,296]{2,1,0:T(8,128)(2,1)}), bf16[16,64,296]{2,1,0:T(8,128)(2,1)}, u32[]{:S(2)}, u32[]{:S(2)}) async-start(bf16[16,64,296]{2,1,0:T(8,128)(2,1)} %copy.268), calls=%async_computation.3 | async-start | bytes 1572864 | tf_op jit(solution)/shard_map/all_to_all | solution.py:129
  29.6 23.1 %copy-start.4 = (bf16[64,64,128]{2,0,1:T(8,128)(2,1)}, bf16[64,64,128]{2,0,1:T(8,128)(2,1)S(1)}, u32[]{:S(2)}) copy-start(bf16[64,64,128]{2,0,1:T(8,128)(2,1)S(1)} %copy.226) | copy-start | bytes 3145732
  32.3 20.3 %copy-start.9 = (bf16[64,64,16]{2,0,1:T(8,128)(2,1)}, bf16[64,64,16]{2,0,1:T(8,128)(2,1)S(1)}, u32[]{:S(2)}) copy-start(bf16[64,64,16]{2,0,1:T(8,128)(2,1)S(1)} %copy.225) | copy-start | bytes 393220
  35.1 17.6 %copy-start.7 = (bf16[64,64,16]{2,0,1:T(8,128)(2,1)}, bf16[64,64,16]{2,0,1:T(8,128)(2,1)S(1)}, u32[]{:S(2)}) copy-start(bf16[64,64,16]{2,0,1:T(8,128)(2,1)S(1)} %copy.227) | copy-start | bytes 393220
  35.7 9.7 %collective-permute-start.2 = (bf16[64,16,160]{2,0,1:T(8,128)(2,1)S(1)}, bf16[64,16,160]{2,0,1:T(8,128)(2,1)S(1)}, u32[]{:S(2)}, u32[]{:S(2)}) collective-permute-start(bf16[64,16,160]{2,0,1:T(8,128)(2,1)S(1)} %get-tuple-element.66), channel_id=1, source_target_pairs={{0,1},{1,2},{2,3},{3,4},{4,5},{5,6},{6,7},{7,8},{8,9},{9,10},{10,1... | collective-permute-start | bytes 983048 | tf_op jit(solution)/shard_map/ppermute | solution.py:15
  39.3 3.5 copy-start.45
  39.3 13.3 %collective-permute-start.3 = (bf16[64,16,160]{2,0,1:T(8,128)(2,1)S(1)}, bf16[64,16,160]{2,0,1:T(8,128)(2,1)S(1)}, u32[]{:S(2)}, u32[]{:S(2)}) collective-permute-start(bf16[64,16,160]{2,0,1:T(8,128)(2,1)S(1)} %get-tuple-element.67), channel_id=1, source_target_pairs={{1,0},{2,1},{3,2},{4,3},{5,4},{6,5},{7,6},{8,7},{9,8},{10,9},{11,1... | collective-permute-start | bytes 983048 | tf_op jit(solution)/shard_map/ppermute | solution.py:18
  55.8 1.6 copy-start.29
  55.9 2.3 copy-start.31
  195.2 52.0 %copy-start.2 = (bf16[64,64,128]{2,0,1:T(8,128)(2,1)}, bf16[64,64,128]{2,0,1:T(8,128)(2,1)S(1)}, u32[]{:S(2)}) copy-start(bf16[64,64,128]{2,0,1:T(8,128)(2,1)S(1)} %fusion.5) | copy-start | bytes 3145732
  199.3 7.2 collective-permute-start.4
  205.2 8.9 collective-permute-start.5
  220.2 27.0 %collective-permute-start.7 = (bf16[64,16,160]{2,0,1:T(8,128)(2,1)}, bf16[64,16,160]{2,0,1:T(8,128)(2,1)}, u32[]{:S(2)}, u32[]{:S(2)}) collective-permute-start(bf16[64,16,160]{2,0,1:T(8,128)(2,1)} %get-tuple-element.62), channel_id=1, source_target_pairs={{1,0},{2,1},{3,2},{4,3},{5,4},{6,5},{7,6},{8,7},{9,8},{10,9},{11,1... | collective-permute-start | bytes 983048 | tf_op jit(solution)/shard_map/ppermute | solution.py:18
  224.1 23.1 %collective-permute-start.6 = (bf16[64,16,160]{2,0,1:T(8,128)(2,1)}, bf16[64,16,160]{2,0,1:T(8,128)(2,1)}, u32[]{:S(2)}, u32[]{:S(2)}) collective-permute-start(bf16[64,16,160]{2,0,1:T(8,128)(2,1)} %get-tuple-element.63), channel_id=1, source_target_pairs={{0,1},{1,2},{2,3},{3,4},{4,5},{5,6},{6,7},{7,8},{8,9},{9,10},{10,1... | collective-permute-start | bytes 983048 | tf_op jit(solution)/shard_map/ppermute | solution.py:15
  233.1 94.7 %all-to-all-start.4 = ((bf16[128,2,1184]{2,1,0:T(2,128)(2,1)}), bf16[128,2,1184]{2,1,0:T(2,128)(2,1)}, u32[]{:S(2)}, u32[]{:S(2)}) async-start(bf16[128,2,1184]{2,1,0:T(2,128)(2,1)} %reshape.289), calls=%async_computation.4 | async-start | bytes 1310720 | tf_op jit(solution)/shard_map/all_to_all | solution.py:136
  244.3 3.0 copy-start.11
  244.3 3.0 copy-start.13
  251.5 1.5 copy-start.25
  251.5 2.4 copy-start.27
  336.5 71.6 %all-to-all-start.5 = ((bf16[8,16,8,296]{3,2,0,1:T(8,128)(2,1)}), bf16[8,16,8,296]{3,2,0,1:T(8,128)(2,1)S(1)}, u32[]{:S(2)}, u32[]{:S(2)}) async-start(bf16[8,16,8,296]{3,2,0,1:T(8,128)(2,1)} %copy.271), calls=%async_computation.5 | async-start | bytes 1572864 | tf_op jit(solution)/shard_map/all_to_all | solution.py:143
  434.1 1.8 copy-start.6
  434.2 2.0 copy-start.17
  502.3 3.0 copy-start.28
  506.3 1.8 copy-start.3
  506.3 1.8 copy-start.14
  508.2 1.8 copy-start.26
  513.2 2.3 copy-start.12
  517.0 11.8 %copy-start.48 = (f32[37]{0:T(128)S(1)}, f32[37]{0:T(128)}, u32[]{:S(2)}) copy-start(f32[37]{0:T(128)} %param.10) | copy-start | bytes 448
  522.8 33.1 %collective-permute-start.9 = (bf16[64,64,16]{1,2,0:T(8,128)(2,1)}, bf16[64,64,16]{1,2,0:T(8,128)(2,1)}, u32[]{:S(2)}, u32[]{:S(2)}) collective-permute-start(bf16[64,64,16]{1,2,0:T(8,128)(2,1)} %copy.276), channel_id=1, source_target_pairs={{16,0},{32,16},{48,32},{64,48},{80,64},{96,80},{112,96},{17,1},{33... | collective-permute-start | bytes 393224 | tf_op jit(solution)/shard_map/ppermute | solution.py:18
  524.1 28.4 %collective-permute-start.8 = (bf16[64,64,16]{1,2,0:T(8,128)(2,1)}, bf16[64,64,16]{1,2,0:T(8,128)(2,1)}, u32[]{:S(2)}, u32[]{:S(2)}) collective-permute-start(bf16[64,64,16]{1,2,0:T(8,128)(2,1)} %copy.275), channel_id=1, source_target_pairs={{0,16},{16,32},{32,48},{48,64},{64,80},{80,96},{96,112},{1,17},{17... | collective-permute-start | bytes 393224 | tf_op jit(solution)/shard_map/ppermute | solution.py:15
  530.4 4.6 copy-start.33
  546.9 301.6 %all-to-all-start = ((f32[16,64,296]{2,1,0:T(8,128)}), f32[16,64,296]{2,1,0:T(8,128)}, u32[]{:S(2)}, u32[]{:S(2)}) async-start(f32[16,64,296]{2,1,0:T(8,128)} %copy.260), calls=%async_computation | async-start | bytes 3145728 | tf_op jit(solution)/shard_map/all_to_all | solution.py:162
  552.3 281.4 %all-reduce.5.cloned.1.call-start = ((), (), s32[]{:S(2)}) async-start(), calls=%async_computation.6 | async-start | bytes 1179648 | tf_op jit(solution)/shard_map/psum | solution.py:238
  559.3 7.5 copy-start.34
  559.3 7.5 copy-start.36
  559.3 8.0 copy-start.23
  559.3 8.0 copy-start.24
  561.2 15.3 %collective-permute-start.11 = (bf16[64,16,160]{2,0,1:T(8,128)(2,1)S(1)}, bf16[64,16,160]{2,0,1:T(8,128)(2,1)S(1)}, u32[]{:S(2)}, u32[]{:S(2)}) collective-permute-start(bf16[64,16,160]{2,0,1:T(8,128)(2,1)S(1)} %get-tuple-element.58), channel_id=1, source_target_pairs={{0,1},{1,2},{2,3},{3,4},{4,5},{5,6},{6,7},{7,8},{8,9},{9,10},{10,1... | collective-permute-start | bytes 983048 | tf_op jit(solution)/shard_map/ppermute | solution.py:15
  564.8 18.9 %collective-permute-start.10 = (bf16[64,16,160]{2,0,1:T(8,128)(2,1)S(1)}, bf16[64,16,160]{2,0,1:T(8,128)(2,1)S(1)}, u32[]{:S(2)}, u32[]{:S(2)}) collective-permute-start(bf16[64,16,160]{2,0,1:T(8,128)(2,1)S(1)} %get-tuple-element.59), channel_id=1, source_target_pairs={{1,0},{2,1},{3,2},{4,3},{5,4},{6,5},{7,6},{8,7},{9,8},{10,9},{11,1... | collective-permute-start | bytes 983048 | tf_op jit(solution)/shard_map/ppermute | solution.py:18
  662.2 2.7 copy-start.32
  665.4 2.4 copy-start.5
  665.4 2.4 copy-start.10
  667.2 1.8 copy-start.30
  673.5 12.3 %copy-start.47 = (f32[9,64,64]{2,1,0:T(8,128)}, f32[9,64,64]{2,1,0:T(8,128)S(1)}, u32[]{:S(2)}) copy-start(f32[9,64,64]{2,1,0:T(8,128)S(1)} %fusion.34) | copy-start | bytes 442372
  679.5 13.4 %collective-permute-start.13 = (bf16[64,64,16]{1,2,0:T(8,128)(2,1)}, bf16[64,64,16]{1,2,0:T(8,128)(2,1)}, u32[]{:S(2)}, u32[]{:S(2)}) collective-permute-start(bf16[64,64,16]{1,2,0:T(8,128)(2,1)} %copy.292), channel_id=1, source_target_pairs={{16,0},{32,16},{48,32},{64,48},{80,64},{96,80},{112,96},{17,1},{33... | collective-permute-start | bytes 393224 | tf_op jit(solution)/shard_map/ppermute | solution.py:18
  680.8 8.8 collective-permute-start.12
  696.3 9.4 copy-start.21
  696.3 9.4 copy-start.22
  699.2 137.9 %collective-permute-start.15 = (bf16[64,16,160]{2,0,1:T(8,128)(2,1)}, bf16[64,16,160]{2,0,1:T(8,128)(2,1)}, u32[]{:S(2)}, u32[]{:S(2)}) collective-permute-start(bf16[64,16,160]{2,0,1:T(8,128)(2,1)} %get-tuple-element.54), channel_id=1, source_target_pairs={{0,1},{1,2},{2,3},{3,4},{4,5},{5,6},{6,7},{7,8},{8,9},{9,10},{10,1... | collective-permute-start | bytes 983048 | tf_op jit(solution)/shard_map/ppermute | solution.py:15
  703.8 133.3 %collective-permute-start.14 = (bf16[64,16,160]{2,0,1:T(8,128)(2,1)}, bf16[64,16,160]{2,0,1:T(8,128)(2,1)}, u32[]{:S(2)}, u32[]{:S(2)}) collective-permute-start(bf16[64,16,160]{2,0,1:T(8,128)(2,1)} %get-tuple-element.55), channel_id=1, source_target_pairs={{1,0},{2,1},{3,2},{4,3},{5,4},{6,5},{7,6},{8,7},{9,8},{10,9},{11,1... | collective-permute-start | bytes 983048 | tf_op jit(solution)/shard_map/ppermute | solution.py:18
  841.9 1.8 copy-start.46
  844.2 2.5 copy-start.39
  852.7 31.3 %all-to-all-start.1 = ((f32[1024,1,296]{2,1,0:T(1,128)}), f32[1024,1,296]{2,1,0:T(1,128)}, u32[]{:S(2)}, u32[]{:S(2)}) async-start(f32[1024,1,296]{2,1,0:T(1,128)} %copy.261), calls=%async_computation.1 | async-start | bytes 3145728 | tf_op jit(solution)/shard_map/all_to_all | solution.py:169
  860.1 2.5 copy-start.42
  862.6 1.6 copy-start.20
  887.0 27.1 %all-to-all-start.2 = ((f32[8,16,8,296]{3,2,0,1:T(8,128)}), f32[8,16,8,296]{3,2,0,1:T(8,128)}, u32[]{:S(2)}, u32[]{:S(2)}) async-start(f32[8,16,8,296]{3,2,0,1:T(8,128)} %copy.263), calls=%async_computation.2 | async-start | bytes 3145728 | tf_op jit(solution)/shard_map/all_to_all | solution.py:176
  895.0 1.6 copy-start.19
  926.2 11.2 %copy-start.37 = (f32[5,8,64,128]{3,2,1,0:T(8,128)S(1)}, f32[5,8,64,128]{3,2,1,0:T(8,128)}, u32[]{:S(2)}) copy-start(f32[5,8,64,128]{3,2,1,0:T(8,128)} %copy.361) | copy-start | bytes 3932164
  926.2 12.2 %copy-start.1 = (bf16[37,64]{1,0:T(8,128)(2,1)S(1)}, bf16[37,64]{1,0:T(8,128)(2,1)}, u32[]{:S(2)}) copy-start(bf16[37,64]{1,0:T(8,128)(2,1)} %param.9) | copy-start | bytes 14212
  (8 other events, 9.2 us)
Sparse Core Ops, SparseCore 0:
  686.0 147.6 all-reduce.4
where the time goes:
time: 954 us; the launch traced here: 946 us
  blocking collectives  393 us (41%)
  waiting for transfers between devices  191 us (20%)
  local copies, waits for them, and re-layouts  156 us (16%)
  starting transfers between devices  88.6 us (9%)
  other arithmetic  55 us (6%)
  matrix products  46.3 us (5%)
  between operations  15.3 us (2%)
    psum x2, blocking collectives, normalize(): totals = lax.psum(jnp.sum(activation, axis=(1, 2)), ('row', 'col'))  134 us
    psum x2, blocking collectives, norm_back(): lax.psum((jnp.sum(gradient, axis=(1, 2)), jnp.sum(gradient * normed, axis...  130 us
    psum x2, blocking collectives, normalize(): lax.psum(jnp.sum(centered * centered, axis=(1, 2)), ('row', 'col'))  129 us
    psum x1, waiting for transfers between devices, on_device(): lax.psum((first_term, second_term, head_term, bias_term), ('row', 'col'))  125 us
    unnamed x117, local copies, waits for them, and re-layouts  38.8 us
    ppermute x8, starting transfers between devices, with_halo(): lax.ppermute(lax.slice_in_dim(block, block.shape[dim] - width, None, axis...  31.6 us
    dot_general x36, matrix products, convolve(): jnp.dot(matrix, window, preferred_element_type=jnp.float32)  25.6 us
    convert_element_type x2, local copies, waits for them, and re-layouts, on_device(): cot_mirror.astype(jnp.float32)  23.2 us
  transfers between devices with their start and end apart: 23, of which 9 were waited for; matrix products, arithmetic and copies ran while one was open for 16% of the time, Pallas kernels for 0%

commit v1 on v0

--- a/solution.py
+++ b/solution.py
@@ -91,7 +91,8 @@
 
 def norm_back(gradient, normed, inverse_std, cell_count):
     first_sum, second_sum = lax.psum(
-        (jnp.sum(gradient, axis=(1, 2)), jnp.sum(gradient * normed, axis=(1, 2))), ("row", "col")
+        lax.psum((jnp.sum(gradient, axis=(1, 2)), jnp.sum(gradient * normed, axis=(1, 2))), "col"),
+        "row",
     )
     first_mean = first_sum / cell_count
     second_mean = second_sum / cell_count

time: 954 us -> 983 us (1.030)
  blocking collectives: 393 us -> 425 us
  starting transfers between devices: 88.6 us -> 99.9 us
    psum x0 -> x3, blocking collectives: none -> 112 us  [the longest x1 76 us: on_device(): lax.psum((first_term, second_term, head_term, bias_term), ('row', 'col'))]
    psum x2, blocking collectives: 130 us -> 50 us  [norm_back(): lax.psum((jnp.sum(gradient, axis=(1, 2)), jnp.sum(gradient * normed, axis...]
    unnamed x117 -> x119, local copies, waits for them, and re-layouts: 38.8 us -> 41.5 us
  transfers between devices with their start and end apart: 23 -> 23, of which waited for: 9 -> 8; matrix products, arithmetic and copies ran while one was open for 16% -> 15% of each run, Pallas kernels for 0% -> 0%
where the time goes in v1:
time: 983 us; the launch traced here: 974 us
  blocking collectives  425 us (43%)
  waiting for transfers between devices  182 us (19%)
  local copies, waits for them, and re-layouts  159 us (16%)
  starting transfers between devices  99.9 us (10%)
  other arithmetic  55.2 us (6%)
  matrix products  39 us (4%)
  between operations  15.4 us (2%)
    psum x2, blocking collectives, normalize(): totals = lax.psum(jnp.sum(activation, axis=(1, 2)), ('row', 'col'))  134 us
    psum x2, blocking collectives, normalize(): lax.psum(jnp.sum(centered * centered, axis=(1, 2)), ('row', 'col'))  129 us
    psum x1, waiting for transfers between devices, on_device(): lax.psum((first_term, second_term, head_term, bias_term), ('row', 'col'))  125 us
    psum x1, blocking collectives, on_device(): lax.psum((first_term, second_term, head_term, bias_term), ('row', 'col'))  76 us
    psum x2, blocking collectives, norm_back(): lax.psum((jnp.sum(gradient, axis=(1, 2)), jnp.sum(gradient * normed, axis...  50 us
    unnamed x119, local copies, waits for them, and re-layouts  41.5 us
    psum x2, blocking collectives, norm_back(): lax.psum(lax.psum((jnp.sum(gradient, axis=(1, 2)), jnp.sum(gradient * nor...  35.5 us
    ppermute x8, starting transfers between devices, with_halo(): lax.ppermute(lax.slice_in_dim(block, block.shape[dim] - width, None, axis...  34.7 us
  transfers between devices with their start and end apart: 23, of which 8 were waited for; matrix products, arithmetic and copies ran while one was open for 15% of the time, Pallas kernels for 0%

profile of v1, /device:TPU:1, one launch (start us, length us, event | category | flops | bytes accessed | tf_op | source)
XLA Modules:
  0.0 974.4 jit_solution(11505383016378026617)
XLA Ops:
  12.6 5.3 collective-permute-start
  21.1 7.8 all-to-all-start.3
  29.6 2.7 copy.225
  32.3 2.7 copy.227
  35.8 3.5 collective-permute-start.2
  45.4 7.2 collective-permute-done.3
  52.7 3.2 maximum_maximum_fusion
  63.5 67.2 %psum.112 = f32[64]{0:T(128)S(1)} all-reduce(f32[64]{0:T(128)S(1)} %get-tuple-element.112), channel_id=1, replica_groups=mesh['row'=8,'col'=16] {'row','col'}, use_global_device_ids=true, to_apply=%region_1.0 | all-reduce | flops 64 | bytes 512 | tf_op jit(solution)/shard_map/psum | solution.py:84
  131.1 63.4 %psum.113 = f32[64]{0:T(128)S(1)} all-reduce(f32[64]{0:T(128)S(1)} %multiply_reduce_fusion.2), channel_id=1, replica_groups=mesh['row'=8,'col'=16] {'row','col'}, use_global_device_ids=true, to_apply=%region_3.0 | all-reduce | flops 64 | bytes 512 | tf_op jit(solution)/shard_map/psum | solution.py:87
  199.2 3.1 collective-permute-start.4
  202.3 2.9 copy.242
  206.5 3.4 copy.243
  209.9 4.2 collective-permute-done.5
  214.1 3.4 copy.244
  217.4 2.8 pad_maximum_fusion.18
  220.2 4.0 collective-permute-start.7
  226.6 3.1 reduce.8
  229.7 3.4 reshape.289
  233.1 11.2 %all-to-all-start.4 = ((bf16[128,2,1184]{2,1,0:T(2,128)(2,1)}), bf16[128,2,1184]{2,1,0:T(2,128)(2,1)}, u32[]{:S(2)}, u32[]{:S(2)}) async-start(bf16[128,2,1184]{2,1,0:T(2,128)(2,1)} %reshape.289), calls=%async_computation.4 | async-start | bytes 1310720 | tf_op jit(solution)/shard_map/all_to_all | solution.py:137
  244.4 2.9 fusion.146
  247.3 4.2 pad_maximum_fusion.1
  260.7 67.2 %psum.114 = f32[64]{0:T(128)S(1)} all-reduce(f32[64]{0:T(128)S(1)} %get-tuple-element.114), channel_id=1, replica_groups=mesh['row'=8,'col'=16] {'row','col'}, use_global_device_ids=true, to_apply=%region_5.6 | all-reduce | flops 64 | bytes 512 | tf_op jit(solution)/shard_map/psum | solution.py:84
  327.9 6.2 reshape.290
  336.6 4.3 all-to-all-start.5
  342.9 65.3 %psum.115 = f32[64]{0:T(128)S(1)} all-reduce(f32[64]{0:T(128)S(1)} %fusion.19), channel_id=1, replica_groups=mesh['row'=8,'col'=16] {'row','col'}, use_global_device_ids=true, to_apply=%region_7.8 | all-reduce | flops 64 | bytes 512 | tf_op jit(solution)/shard_map/psum | solution.py:87
  409.5 12.2 %reshape.288 = f32[128,8,37,8]{3,2,1,0:T(8,128)} reshape(f32[16,8,1,8,296]{4,3,1,0,2:T(8,128)} %convert_bitcast_fusion) | data formatting | bytes 2424832 | tf_op jit(solution)/shard_map/convert_element_type | solution.py:212
  421.7 11.1 %copy.273 = f32[37,8,8,128]{3,2,1,0:T(8,128)S(1)} copy(f32[37,8,8,128]{2,0,1,3:T(8,128)} %bitcast.528) | data formatting | bytes 2424832 | tf_op jit(solution)/shard_map/convert_element_type | solution.py:212
  436.3 3.2 fusion.228
  439.5 27.4 %all-reduce.3 = (f32[64]{0:T(128)S(1)}, f32[64]{0:T(128)S(1)}) all-reduce(f32[64]{0:T(128)S(1)} %get-tuple-element.39, f32[64]{0:T(128)S(1)} %get-tuple-element.38), channel_id=1, replica_groups=mesh['row'=8,'col'=16] {'col'}, use_global_device_ids=true, to_apply=%region_12.13 | all-reduce | flops 128 | bytes 1024 | tf_op jit(solution)/shard_map/psum | solution.py:94
  466.9 17.8 %all-reduce.5 = (f32[64]{0:T(128)S(1)}, f32[64]{0:T(128)S(1)}) all-reduce(f32[64]{0:T(128)S(1)} %get-tuple-element.46, f32[64]{0:T(128)S(1)} %get-tuple-element.47), channel_id=1, replica_groups=mesh['row'=8,'col'=16] {'row'}, use_global_device_ids=true, to_apply=%region_13.14 | all-reduce | flops 128 | bytes 1024 | tf_op jit(solution)/shard_map/psum | solution.py:93
  484.7 2.9 multiply_convert_fusion.1
  498.7 2.9 copy.275
  501.6 2.9 copy.276
  505.8 4.7 collective-permute-start.8
  510.5 3.7 copy.258
  514.3 5.2 copy.259
  519.4 3.1 copy.260
  522.5 9.9 %all-to-all-start = ((f32[16,64,296]{2,1,0:T(8,128)}), f32[16,64,296]{2,1,0:T(8,128)}, u32[]{:S(2)}, u32[]{:S(2)}) async-start(f32[16,64,296]{2,1,0:T(8,128)} %copy.260), calls=%async_computation | async-start | bytes 3145728 | tf_op jit(solution)/shard_map/all_to_all | solution.py:163
  532.5 76.0 %all-reduce = (f32[37,64]{1,0:T(8,128)S(1)}, f32[37]{0:T(128)S(1)}) all-reduce(f32[37,64]{1,0:T(8,128)S(1)} %convolution_bitcast_fusion.23, f32[37]{0:T(128)S(1)} %get-tuple-element.52), channel_id=1, replica_groups=mesh['row'=8,'col'=16] {'row','col'}, use_global_device_ids=true, to_apply=%region_22.23 | all-reduce | flops 2405 | bytes 19240 | tf_op jit(solution)/shard_map/psum | solution.py:239
  609.1 3.4 copy.277
  612.5 3.4 copy.278
  617.8 3.0 collective-permute-start.11
  626.9 7.2 collective-permute-done.10
  634.2 3.2 maximum_maximum_fusion.2
  645.4 22.6 %all-reduce.2 = (f32[64]{0:T(128)S(1)}, f32[64]{0:T(128)S(1)}) all-reduce(f32[64]{0:T(128)S(1)} %get-tuple-element.37, f32[64]{0:T(128)S(1)} %get-tuple-element.36), channel_id=1, replica_groups=mesh['row'=8,'col'=16] {'col'}, use_global_device_ids=true, to_apply=%region_18.19 | all-reduce | flops 128 | bytes 1024 | tf_op jit(solution)/shard_map/psum | solution.py:94
  668.1 17.7 %all-reduce.4 = (f32[64]{0:T(128)S(1)}, f32[64]{0:T(128)S(1)}) all-reduce(f32[64]{0:T(128)S(1)} %get-tuple-element.44, f32[64]{0:T(128)S(1)} %get-tuple-element.45), channel_id=1, replica_groups=mesh['row'=8,'col'=16] {'row'}, use_global_device_ids=true, to_apply=%region_19.20 | all-reduce | flops 128 | bytes 1024 | tf_op jit(solution)/shard_map/psum | solution.py:93
  685.8 2.7 fusion.10
  696.5 2.9 copy.291
  699.5 2.9 copy.292
  703.7 4.7 collective-permute-start.12
  711.3 3.4 copy.293
  714.7 3.4 copy.294
  718.0 2.9 pad_maximum_fusion.12
  720.9 8.5 collective-permute-start.15
  729.4 5.8 collective-permute-start.14
  737.8 124.7 %all-reduce.8.cloned.1.call-done = (f32[9,64,64]{2,1,0:T(8,128)}, f32[9,64,64]{2,1,0:T(8,128)}) async-done(((f32[9,64,64]{2,1,0:T(8,128)}, f32[9,64,64]{2,1,0:T(8,128)}), (f32[9,64,64]{2,1,0:T(8,128)}, f32[9,64,64]{2,1,0:T(8,128)})) %all-reduce.8.cloned.1.call-update) | async-done | bytes 294928 | tf_op jit(solution)/shard_map/psum | solution.py:239
  865.9 5.0 maximum_maximum_fusion.3
  877.5 4.2 copy.261
  881.7 7.1 all-to-all-start.1
  894.8 18.1 %all-to-all-done.1 = f32[1024,1,296]{2,1,0:T(1,128)} async-done(((f32[1024,1,296]{2,1,0:T(1,128)}), f32[1024,1,296]{2,1,0:T(1,128)}, u32[]{:S(2)}, u32[]{:S(2)}) %all-to-all-start.1) | async-done | bytes 1212448 | tf_op jit(solution)/shard_map/all_to_all | solution.py:170
  915.8 5.7 all-to-all-start.2
  927.6 15.3 %all-to-all-done.2 = f32[8,16,8,296]{3,2,0,1:T(8,128)} async-done(((f32[8,16,8,296]{3,2,0,1:T(8,128)}), f32[8,16,8,296]{3,2,0,1:T(8,128)}, u32[]{:S(2)}, u32[]{:S(2)}) %all-to-all-start.2) | async-done | bytes 1212448 | tf_op jit(solution)/shard_map/all_to_all | solution.py:177
  942.9 12.2 %reshape.287 = f32[128,8,37,8]{3,2,1,0:T(8,128)} reshape(f32[16,8,1,8,296]{4,3,1,0,2:T(8,128)} %bitcast.32) | data formatting | bytes 2424832 | tf_op jit(solution)/shard_map/reshape | solution.py:122
  955.1 11.2 %copy.265 = f32[37,8,8,128]{3,2,1,0:T(8,128)S(1)} copy(f32[37,8,8,128]{2,0,1,3:T(8,128)} %bitcast.529) | data formatting | bytes 2424832 | tf_op jit(solution)/shard_map/transpose | solution.py:122
  (234 shorter events, 120.4 us)
Async XLA Ops:
  7.2 427.9 %copy-start = (bf16[37,64]{1,0:T(8,128)(2,1)S(1)}, bf16[37,64]{1,0:T(8,128)(2,1)}, u32[]{:S(2)}) copy-start(bf16[37,64]{1,0:T(8,128)(2,1)} %param.9) | copy-start | bytes 14212
  9.2 8.7 copy-start.43
  10.3 22.1 %collective-permute-start.1 = (bf16[64,64,16]{1,2,0:T(8,128)(2,1)}, bf16[64,64,16]{1,2,0:T(8,128)(2,1)}, u32[]{:S(2)}, u32[]{:S(2)}) collective-permute-start(bf16[64,64,16]{1,2,0:T(8,128)(2,1)} %copy.320), channel_id=1, source_target_pairs={{16,0},{32,16},{48,32},{64,48},{80,64},{96,80},{112,96},{17,1},{33... | collective-permute-start | bytes 393224 | tf_op jit(solution)/shard_map/ppermute | solution.py:18
  12.6 16.9 %collective-permute-start = (bf16[64,64,16]{1,2,0:T(8,128)(2,1)}, bf16[64,64,16]{1,2,0:T(8,128)(2,1)}, u32[]{:S(2)}, u32[]{:S(2)}) collective-permute-start(bf16[64,64,16]{1,2,0:T(8,128)(2,1)} %copy.319), channel_id=1, source_target_pairs={{0,16},{16,32},{32,48},{48,64},{64,80},{80,96},{96,112},{1,17},{17... | collective-permute-start | bytes 393224 | tf_op jit(solution)/shard_map/ppermute | solution.py:15
  19.6 9.2 copy-start.15
  21.1 205.0 %all-to-all-start.3 = ((bf16[16,64,296]{2,1,0:T(8,128)(2,1)}), bf16[16,64,296]{2,1,0:T(8,128)(2,1)}, u32[]{:S(2)}, u32[]{:S(2)}) async-start(bf16[16,64,296]{2,1,0:T(8,128)(2,1)} %copy.268), calls=%async_computation.3 | async-start | bytes 1572864 | tf_op jit(solution)/shard_map/all_to_all | solution.py:130
  29.6 23.1 %copy-start.4 = (bf16[64,64,128]{2,0,1:T(8,128)(2,1)}, bf16[64,64,128]{2,0,1:T(8,128)(2,1)S(1)}, u32[]{:S(2)}) copy-start(bf16[64,64,128]{2,0,1:T(8,128)(2,1)S(1)} %copy.226) | copy-start | bytes 3145732
  32.3 20.3 %copy-start.9 = (bf16[64,64,16]{2,0,1:T(8,128)(2,1)}, bf16[64,64,16]{2,0,1:T(8,128)(2,1)S(1)}, u32[]{:S(2)}) copy-start(bf16[64,64,16]{2,0,1:T(8,128)(2,1)S(1)} %copy.225) | copy-start | bytes 393220
  35.1 17.6 %copy-start.7 = (bf16[64,64,16]{2,0,1:T(8,128)(2,1)}, bf16[64,64,16]{2,0,1:T(8,128)(2,1)S(1)}, u32[]{:S(2)}) copy-start(bf16[64,64,16]{2,0,1:T(8,128)(2,1)S(1)} %copy.227) | copy-start | bytes 393220
  35.8 9.7 collective-permute-start.2
  39.3 3.5 copy-start.45
  39.3 13.3 %collective-permute-start.3 = (bf16[64,16,160]{2,0,1:T(8,128)(2,1)S(1)}, bf16[64,16,160]{2,0,1:T(8,128)(2,1)S(1)}, u32[]{:S(2)}, u32[]{:S(2)}) collective-permute-start(bf16[64,16,160]{2,0,1:T(8,128)(2,1)S(1)} %get-tuple-element.71), channel_id=1, source_target_pairs={{1,0},{2,1},{3,2},{4,3},{5,4},{6,5},{7,6},{8,7},{9,8},{10,9},{11,1... | collective-permute-start | bytes 983048 | tf_op jit(solution)/shard_map/ppermute | solution.py:18
  55.8 1.6 copy-start.29
  55.9 2.3 copy-start.31
  60.7 1.2 copy-start.16
  195.1 52.2 %copy-start.2 = (bf16[64,64,128]{2,0,1:T(8,128)(2,1)}, bf16[64,64,128]{2,0,1:T(8,128)(2,1)S(1)}, u32[]{:S(2)}) copy-start(bf16[64,64,128]{2,0,1:T(8,128)(2,1)S(1)} %fusion.5) | copy-start | bytes 3145732
  199.2 7.3 collective-permute-start.4
  205.2 8.9 collective-permute-start.5
  220.2 27.1 %collective-permute-start.7 = (bf16[64,16,160]{2,0,1:T(8,128)(2,1)}, bf16[64,16,160]{2,0,1:T(8,128)(2,1)}, u32[]{:S(2)}, u32[]{:S(2)}) collective-permute-start(bf16[64,16,160]{2,0,1:T(8,128)(2,1)} %get-tuple-element.66), channel_id=1, source_target_pairs={{1,0},{2,1},{3,2},{4,3},{5,4},{6,5},{7,6},{8,7},{9,8},{10,9},{11,1... | collective-permute-start | bytes 983048 | tf_op jit(solution)/shard_map/ppermute | solution.py:18
  224.2 23.1 %collective-permute-start.6 = (bf16[64,16,160]{2,0,1:T(8,128)(2,1)}, bf16[64,16,160]{2,0,1:T(8,128)(2,1)}, u32[]{:S(2)}, u32[]{:S(2)}) collective-permute-start(bf16[64,16,160]{2,0,1:T(8,128)(2,1)} %get-tuple-element.67), channel_id=1, source_target_pairs={{0,1},{1,2},{2,3},{3,4},{4,5},{5,6},{6,7},{7,8},{8,9},{9,10},{10,1... | collective-permute-start | bytes 983048 | tf_op jit(solution)/shard_map/ppermute | solution.py:15
  233.1 94.7 %all-to-all-start.4 = ((bf16[128,2,1184]{2,1,0:T(2,128)(2,1)}), bf16[128,2,1184]{2,1,0:T(2,128)(2,1)}, u32[]{:S(2)}, u32[]{:S(2)}) async-start(bf16[128,2,1184]{2,1,0:T(2,128)(2,1)} %reshape.289), calls=%async_computation.4 | async-start | bytes 1310720 | tf_op jit(solution)/shard_map/all_to_all | solution.py:137
  244.4 3.0 copy-start.11
  244.4 3.0 copy-start.13
  251.5 1.5 copy-start.25
  251.5 2.4 copy-start.27
  336.6 71.6 %all-to-all-start.5 = ((bf16[8,16,8,296]{3,2,0,1:T(8,128)(2,1)}), bf16[8,16,8,296]{3,2,0,1:T(8,128)(2,1)S(1)}, u32[]{:S(2)}, u32[]{:S(2)}) async-start(bf16[8,16,8,296]{3,2,0,1:T(8,128)(2,1)} %copy.271), calls=%async_computation.5 | async-start | bytes 1572864 | tf_op jit(solution)/shard_map/all_to_all | solution.py:144
  434.3 1.8 copy-start.6
  434.3 2.0 copy-start.17
  484.7 3.0 copy-start.28
  488.2 1.9 copy-start.34
  488.2 1.9 copy-start.36
  488.2 2.4 copy-start.3
  488.2 2.8 copy-start.14
  490.0 1.9 copy-start.26
  494.6 1.4 copy-start.49
  496.0 2.7 copy-start.47
  504.5 108.0 %collective-permute-start.9 = (bf16[64,64,16]{1,2,0:T(8,128)(2,1)}, bf16[64,64,16]{1,2,0:T(8,128)(2,1)}, u32[]{:S(2)}, u32[]{:S(2)}) collective-permute-start(bf16[64,64,16]{1,2,0:T(8,128)(2,1)} %copy.276), channel_id=1, source_target_pairs={{16,0},{32,16},{48,32},{64,48},{80,64},{96,80},{112,96},{17,1},{33... | collective-permute-start | bytes 393224 | tf_op jit(solution)/shard_map/ppermute | solution.py:18
  505.8 103.3 %collective-permute-start.8 = (bf16[64,64,16]{1,2,0:T(8,128)(2,1)}, bf16[64,64,16]{1,2,0:T(8,128)(2,1)}, u32[]{:S(2)}, u32[]{:S(2)}) collective-permute-start(bf16[64,64,16]{1,2,0:T(8,128)(2,1)} %copy.275), channel_id=1, source_target_pairs={{0,16},{16,32},{32,48},{48,64},{64,80},{80,96},{96,112},{1,17},{17... | collective-permute-start | bytes 393224 | tf_op jit(solution)/shard_map/ppermute | solution.py:15
  522.5 355.0 %all-to-all-start = ((f32[16,64,296]{2,1,0:T(8,128)}), f32[16,64,296]{2,1,0:T(8,128)}, u32[]{:S(2)}, u32[]{:S(2)}) async-start(f32[16,64,296]{2,1,0:T(8,128)} %copy.260), calls=%async_computation | async-start | bytes 3145728 | tf_op jit(solution)/shard_map/all_to_all | solution.py:163
  532.4 330.1 %all-reduce.8.cloned.1.call-start = ((), (), s32[]{:S(2)}) async-start(), calls=%async_computation.6 | async-start | bytes 1179648 | tf_op jit(solution)/shard_map/psum | solution.py:239
  615.9 7.4 copy-start.23
  615.9 7.4 copy-start.24
  617.8 9.1 collective-permute-start.11
  620.8 13.4 %collective-permute-start.10 = (bf16[64,16,160]{2,0,1:T(8,128)(2,1)S(1)}, bf16[64,16,160]{2,0,1:T(8,128)(2,1)S(1)}, u32[]{:S(2)}, u32[]{:S(2)}) collective-permute-start(bf16[64,16,160]{2,0,1:T(8,128)(2,1)S(1)} %get-tuple-element.63), channel_id=1, source_target_pairs={{1,0},{2,1},{3,2},{4,3},{5,4},{6,5},{7,6},{8,7},{9,8},{10,9},{11,1... | collective-permute-start | bytes 983048 | tf_op jit(solution)/shard_map/ppermute | solution.py:18
  685.8 2.7 copy-start.32
  688.9 1.8 copy-start.5
  688.9 1.8 copy-start.10
  690.7 1.7 copy-start.30
  702.4 12.3 %collective-permute-start.13 = (bf16[64,64,16]{1,2,0:T(8,128)(2,1)}, bf16[64,64,16]{1,2,0:T(8,128)(2,1)}, u32[]{:S(2)}, u32[]{:S(2)}) collective-permute-start(bf16[64,64,16]{1,2,0:T(8,128)(2,1)} %copy.292), channel_id=1, source_target_pairs={{16,0},{32,16},{48,32},{64,48},{80,64},{96,80},{112,96},{17,1},{33... | collective-permute-start | bytes 393224 | tf_op jit(solution)/shard_map/ppermute | solution.py:18
  703.7 7.6 collective-permute-start.12
  718.0 17.2 %copy-start.21 = (bf16[64,64,16]{2,0,1:T(8,128)(2,1)S(1)}, bf16[64,64,16]{2,0,1:T(8,128)(2,1)}, u32[]{:S(2)}) copy-start(bf16[64,64,16]{2,0,1:T(8,128)(2,1)} %copy.293) | copy-start | bytes 393220
  718.0 17.3 %copy-start.22 = (bf16[64,64,16]{2,0,1:T(8,128)(2,1)S(1)}, bf16[64,64,16]{2,0,1:T(8,128)(2,1)}, u32[]{:S(2)}) copy-start(bf16[64,64,16]{2,0,1:T(8,128)(2,1)} %copy.294) | copy-start | bytes 393220
  720.9 145.0 %collective-permute-start.15 = (bf16[64,16,160]{2,0,1:T(8,128)(2,1)}, bf16[64,16,160]{2,0,1:T(8,128)(2,1)}, u32[]{:S(2)}, u32[]{:S(2)}) collective-permute-start(bf16[64,16,160]{2,0,1:T(8,128)(2,1)} %get-tuple-element.58), channel_id=1, source_target_pairs={{0,1},{1,2},{2,3},{3,4},{4,5},{5,6},{6,7},{7,8},{8,9},{9,10},{10,1... | collective-permute-start | bytes 983048 | tf_op jit(solution)/shard_map/ppermute | solution.py:15
  729.4 136.5 %collective-permute-start.14 = (bf16[64,16,160]{2,0,1:T(8,128)(2,1)}, bf16[64,16,160]{2,0,1:T(8,128)(2,1)}, u32[]{:S(2)}, u32[]{:S(2)}) collective-permute-start(bf16[64,16,160]{2,0,1:T(8,128)(2,1)} %get-tuple-element.59), channel_id=1, source_target_pairs={{1,0},{2,1},{3,2},{4,3},{5,4},{6,5},{7,6},{8,7},{9,8},{10,9},{11,1... | collective-permute-start | bytes 983048 | tf_op jit(solution)/shard_map/ppermute | solution.py:18
  870.9 1.8 copy-start.46
  873.2 2.5 copy-start.39
  881.7 31.2 %all-to-all-start.1 = ((f32[1024,1,296]{2,1,0:T(1,128)}), f32[1024,1,296]{2,1,0:T(1,128)}, u32[]{:S(2)}, u32[]{:S(2)}) async-start(f32[1024,1,296]{2,1,0:T(1,128)} %copy.261), calls=%async_computation.1 | async-start | bytes 3145728 | tf_op jit(solution)/shard_map/all_to_all | solution.py:170
  888.8 2.5 copy-start.42
  891.3 1.6 copy-start.20
  892.9 1.4 copy-start.41
  915.8 27.1 %all-to-all-start.2 = ((f32[8,16,8,296]{3,2,0,1:T(8,128)}), f32[8,16,8,296]{3,2,0,1:T(8,128)}, u32[]{:S(2)}, u32[]{:S(2)}) async-start(f32[8,16,8,296]{3,2,0,1:T(8,128)} %copy.263), calls=%async_computation.2 | async-start | bytes 3145728 | tf_op jit(solution)/shard_map/all_to_all | solution.py:177
  924.0 1.6 copy-start.19
  955.1 11.2 %copy-start.37 = (f32[5,8,64,128]{3,2,1,0:T(8,128)S(1)}, f32[5,8,64,128]{3,2,1,0:T(8,128)}, u32[]{:S(2)}) copy-start(f32[5,8,64,128]{3,2,1,0:T(8,128)} %copy.361) | copy-start | bytes 3932164
  955.1 12.2 %copy-start.1 = (bf16[37,64]{1,0:T(8,128)(2,1)S(1)}, bf16[37,64]{1,0:T(8,128)(2,1)}, u32[]{:S(2)}) copy-start(bf16[37,64]{1,0:T(8,128)(2,1)} %param.9) | copy-start | bytes 14212
  (9 other events, 9.7 us)
Sparse Core Ops, SparseCore 0:
  711.4 151.1 all-reduce.7
